TPU v7x, 32 devices: a whole 2x2x4 slice. The times are simulated.
32 devices in a mesh: coef: 16 (over z, y, x), rot: 2 (over core).
Axes of the slice: x: 2, y: 2, z: 4, core: 2. Of those that a mesh axis runs over, the one named last changes fastest.
Arguments:
- features: float32 [256, 47872], P(None, 'coef'), may hold values from -200 to 200
- table: float32 [2048, 47872], P('rot', 'coef'), may hold values from -16 to 16
- targets: float32 [256, 2048], P('coef', 'rot'), may hold values from 0 to 1
Outputs:
- grad_features: float32 [256, 47872], P('rot', 'coef')
- grad_table: float32 [2048, 47872], P('rot', 'coef')
All inputs are finite; a program needn't handle non-finite values.
Results may differ from a plain program's by a relative error of at most 0.0003.
Values sent between devices are 32-bit elements; how exact they have to be, the bound alone decides.
No kernel may reach another device: no remote copies, remote signals or barrier semaphores. Data moves between devices by JAX's collectives and lax.ppermute only.
A program may use at most 64 MiB of HBM per device.

v0:
```python
import math
import jax
import jax.numpy as jnp
from jax import lax
from jax.sharding import PartitionSpec as P

K = 47872
logit_gain = 4.0
loss_scale = 64.0


def on_device(features, table, targets):
    scale = logit_gain / math.sqrt(K)
    partial_value = lax.dot_general(
        features,
        table,
        (((1,), (1,)), ((), ())),
        precision=lax.Precision.HIGHEST,
        preferred_element_type=jnp.float32,
    )
    summed = lax.psum_scatter(partial_value, "coef", scatter_dimension=0, tiled=True)
    scores = scale * summed
    local_max = jnp.max(scores, axis=1)
    row_max = lax.pmax(local_max, "rot")
    expo = jnp.exp(scores - row_max[:, None])
    row_total = lax.psum(jnp.sum(expo, axis=1), "rot")
    probs = expo / row_total[:, None]
    grad_scores = loss_scale * (probs - targets)
    piece = lax.all_gather(grad_scores, "coef", axis=0, tiled=True)
    table_part = lax.dot_general(
        piece,
        features,
        (((0,), (0,)), ((), ())),
        precision=lax.Precision.HIGHEST,
        preferred_element_type=jnp.float32,
    )
    feature_part = jnp.dot(
        piece, table, precision=lax.Precision.HIGHEST, preferred_element_type=jnp.float32
    )
    grad_features = scale * lax.psum_scatter(feature_part, "rot", scatter_dimension=0, tiled=True)
    grad_table = scale * table_part
    return (grad_features, grad_table)


def solution(mesh):
    return jax.shard_map(
        on_device,
        mesh=mesh,
        in_specs=(P(None, "coef"), P("rot", "coef"), P("coef", "rot")),
        out_specs=(P("rot", "coef"), P("rot", "coef")),
        check_vma=False,
    )
```

profile of v0, /device:TPU:0, one launch (start us, length us, event | category | flops | bytes accessed | tf_op | source)
XLA Modules:
  0.0 202.1 jit_solution(17302437431089537872)
XLA Ops:
  7.2 0.0 copy-start
  7.2 0.0 copy-start.1
  7.2 0.0 reduce-scatter.3.cloned.1.call-start
  7.2 1.8 copy-done
  9.0 14.6 %fusion.1 = f32[256,1024]{1,0:T(8,128)} fusion(f32[256,2992]{0,1:T(8,128)S(1)} %copy-done, f32[1024,2992]{0,1:T(8,128)} %param.4), kind=kOutput, calls=%fused_computation.6 | convolution fusion | flops 9412018176 | bytes 16367616 | tf_op jit(solution)/shard_map/dot_general | solution.py:14
  23.6 0.0 reduce-scatter.3.cloned.1.call-update
  23.7 0.0 all-gather.2.cloned.1.call-start
  23.7 81.6 %reduce-scatter.3.cloned.1.call-done = f32[16,1024]{1,0:T(8,128)} async-done(((f32[256,1024]{1,0:T(8,128)}), f32[16,1024]{1,0:T(8,128)}) %reduce-scatter.3.cloned.1.call-update) | async-done | bytes 65552 | tf_op jit(solution)/shard_map/reduce_scatter | solution.py:21
  105.3 1.0 multiply_reduce_fusion
  106.3 2.5 %pmax.7 = f32[16]{0:T(128)S(1)} all-reduce(f32[16]{0:T(128)S(1)} %multiply_reduce_fusion), channel_id=1, replica_groups=mesh['coef'=16,'rot'=2] {'rot'}, use_global_device_ids=true, to_apply=%region_2.0 | all-reduce | flops 16 | bytes 128 | tf_op jit(solution)/shard_map/pmax | solution.py:24
  108.8 1.0 fusion
  109.8 2.5 %psum.7 = f32[16]{0:T(128)S(1)} all-reduce(f32[16]{0:T(128)S(1)} %fusion), channel_id=1, replica_groups=mesh['coef'=16,'rot'=2] {'rot'}, use_global_device_ids=true, to_apply=%region_4.0 | all-reduce | flops 16 | bytes 128 | tf_op jit(solution)/shard_map/psum | solution.py:26
  112.3 0.0 copy-done.1
  112.3 1.6 subtract_multiply_fusion
  113.8 0.0 all-gather.2.cloned.1.call-update
  113.8 0.2 reduce-scatter.5.cloned.1.call-start
  114.1 51.3 %all-gather.2.cloned.1.call-done = f32[256,1024]{1,0:T(8,128)} async-done(((f32[16,1024]{1,0:T(8,128)}), f32[256,1024]{1,0:T(8,128)}) %all-gather.2.cloned.1.call-update) | async-done | bytes 1048592 | tf_op jit(solution)/shard_map/all_gather | solution.py:29
  165.4 13.5 %fusion.2 = f32[256,2992]{0,1:T(8,128)} fusion(f32[256,1024]{1,0:T(8,128)} %all-gather.2.cloned.1.call-done, f32[1024,2992]{0,1:T(8,128)} %param.4), kind=kOutput, calls=%fused_computation.7 | convolution fusion | flops 9412018176 | bytes 16367616 | tf_op jit(solution)/shard_map/dot_general | solution.py:37
  178.9 0.0 reduce-scatter.5.cloned.1.call-update
  178.9 14.0 %convolution_multiply_fusion = f32[1024,2992]{0,1:T(8,128)} fusion(f32[256,1024]{1,0:T(8,128)} %all-gather.2.cloned.1.call-done, f32[256,2992]{0,1:T(8,128)S(1)} %copy-done), kind=kOutput, calls=%fused_computation | convolution fusion | flops 9415081984 | bytes 16367616 | tf_op jit(solution)/shard_map/dot_general | solution.py:30
  192.9 0.0 reduce-scatter.5.cloned.1.call-done
  192.9 2.7 %broadcast_multiply_fusion = f32[128,2992]{0,1:T(8,128)} fusion(f32[128,2992]{0,1:T(8,128)} %reduce-scatter.5.cloned.1.call-done), kind=kLoop, calls=%fused_computation.1 | loop fusion | flops 382976 | bytes 3063808 | tf_op jit(solution)/shard_map/mul | solution.py:40
Async XLA Ops:
  7.2 1.9 copy-start
  7.2 105.1 %copy-start.1 = (f32[16,1024]{1,0:T(8,128)S(1)}, f32[16,1024]{1,0:T(8,128)}, u32[]{:S(2)}) copy-start(f32[16,1024]{1,0:T(8,128)} %param.5) | copy-start | bytes 196612
  7.2 98.1 %reduce-scatter.3.cloned.1.call-start = ((), (), s32[]{:S(2)}) async-start(), calls=%async_computation.2 | async-start | bytes 1114112 | tf_op jit(solution)/shard_map/reduce_scatter | solution.py:21
  23.7 141.8 %all-gather.2.cloned.1.call-start = ((), (), s32[]{:S(2)}) async-start(), calls=%async_computation.3 | async-start | bytes 1114112 | tf_op jit(solution)/shard_map/all_gather | solution.py:29
  113.8 79.1 %reduce-scatter.5.cloned.1.call-start = ((), (), s32[]{:S(2)}) async-start(), calls=%async_computation.4 | async-start | bytes 4595712 | tf_op jit(solution)/shard_map/reduce_scatter | solution.py:40
Sparse Core Ops, SparseCore 0:
  23.8 81.4 reduce-scatter.2
  114.0 51.4 all-gather.1
  179.0 9.6 reduce-scatter.4
where the time goes:
time: 202 us
  waiting for transfers between devices  133 us (66%)
  matrix products  42.1 us (21%)
  between operations  13.8 us (7%)
  other arithmetic  6.2 us (3%)
  blocking collectives  4.93 us (2%)
    reduce_scatter x1, waiting for transfers between devices, on_device(): lax.psum_scatter(partial_value, 'coef', scatter_dimension=0, tiled=True)  81.6 us
    all_gather x1, waiting for transfers between devices, on_device(): piece = lax.all_gather(grad_scores, 'coef', axis=0, tiled=True)  51.3 us
    dot_general x1, matrix products, on_device(): lax.dot_general(features, table, (((1,), (1,)), ((), ())), precision=lax....  14.6 us
    dot_general x1, matrix products, on_device(): lax.dot_general(piece, features, (((0,), (0,)), ((), ())), precision=lax....  14 us
    dot_general x1, matrix products, on_device(): jnp.dot(piece, table, precision=lax.Precision.HIGHEST, preferred_element_...  13.5 us
  transfers between devices with their start and end apart: 3, of which 2 were waited for; matrix products, arithmetic and copies ran while one was open for 7% of the time, Pallas kernels for 0%

commit v1 on v0

--- a/solution.py
+++ b/solution.py
@@ -26,7 +26,13 @@
     row_total = lax.psum(jnp.sum(expo, axis=1), "rot")
     probs = expo / row_total[:, None]
     grad_scores = loss_scale * (probs - targets)
-    piece = lax.all_gather(grad_scores, "coef", axis=0, tiled=True)
+    size = lax.axis_size("coef")
+    block, tiles = (grad_scores, [grad_scores])
+    for _ in range(size - 1):
+        block = lax.ppermute(block, "coef", [(i, (i + 1) % size) for i in range(size)])
+        tiles.insert(0, block)
+    line = jnp.concatenate(tiles, axis=0)
+    piece = jnp.roll(line, (lax.axis_index("coef") + 1) * grad_scores.shape[0], axis=0)
     table_part = lax.dot_general(
         piece,
         features,

time: 202 us -> 287 us (1.42)
  waiting for transfers between devices: 133 us -> 201 us
  local copies, waits for them, and re-layouts: 1.81 us -> 17 us
    ppermute x0 -> x15, waiting for transfers between devices: none -> 120 us  [on_device(): lax.ppermute(block, 'coef', [(i, (i + 1) % size) for i in range(size)])]
    all_gather x1 -> x0, waiting for transfers between devices: 51.3 us -> none  [on_device(): piece = lax.all_gather(grad_scores, 'coef', axis=0, tiled=True)]
    unnamed x4 -> x65, local copies, waits for them, and re-layouts: 1.81 us -> 17 us
  transfers between devices with their start and end apart: 3 -> 17, of which waited for: 2 -> 16; matrix products, arithmetic and copies ran while one was open for 7% -> 5% of each run, Pallas kernels for 0% -> 0%
where the time goes in v1:
time: 287 us; the launch traced here: 286 us
  waiting for transfers between devices  201 us (70%)
  matrix products  42.8 us (15%)
  local copies, waits for them, and re-layouts  17 us (6%)
  between operations  14.4 us (5%)
  other arithmetic  5.58 us (2%)
  blocking collectives  4.93 us (2%)
    ppermute x15, waiting for transfers between devices, on_device(): lax.ppermute(block, 'coef', [(i, (i + 1) % size) for i in range(size)])  120 us
    reduce_scatter x1, waiting for transfers between devices, on_device(): lax.psum_scatter(partial_value, 'coef', scatter_dimension=0, tiled=True)  81.6 us
    unnamed x65, local copies, waits for them, and re-layouts  17 us
    dot_general x1, matrix products, on_device(): lax.dot_general(features, table, (((1,), (1,)), ((), ())), precision=lax....  14.6 us
    dot_general x1, matrix products, on_device(): jnp.dot(piece, table, precision=lax.Precision.HIGHEST, preferred_element_...  14.2 us
    dot_general x1, matrix products, on_device(): lax.dot_general(piece, features, (((0,), (0,)), ((), ())), precision=lax....  14 us
  transfers between devices with their start and end apart: 17, of which 16 were waited for; matrix products, arithmetic and copies ran while one was open for 5% of the time, Pallas kernels for 0%

profile of v1, /device:TPU:0, one launch (start us, length us, event | category | flops | bytes accessed | tf_op | source)
XLA Modules:
  0.0 286.2 jit_solution(15123278184882092521)
XLA Ops:
  7.2 1.8 copy-done
  9.0 14.6 %fusion.6 = f32[256,1024]{1,0:T(8,128)} fusion(f32[256,2992]{0,1:T(8,128)S(1)} %copy-done, f32[1024,2992]{0,1:T(8,128)} %param.4), kind=kOutput, calls=%fused_computation.43 | convolution fusion | flops 9412018176 | bytes 16367616 | tf_op jit(solution)/shard_map/dot_general | solution.py:14
  23.7 81.6 %reduce-scatter.3.cloned.1.call-done = f32[16,1024]{1,0:T(8,128)} async-done(((f32[256,1024]{1,0:T(8,128)}), f32[16,1024]{1,0:T(8,128)}) %reduce-scatter.3.cloned.1.call-update) | async-done | bytes 65552 | tf_op jit(solution)/shard_map/reduce_scatter | solution.py:21
  105.3 1.0 multiply_reduce_fusion
  106.3 2.5 pmax.7
  108.8 1.0 fusion.3
  109.8 2.5 psum.7
  112.3 0.9 subtract_multiply_fusion
  113.3 7.8 %collective-permute-done = f32[16,1024]{1,0:T(8,128)S(1)} collective-permute-done((f32[16,1024]{1,0:T(8,128)S(1)}, f32[16,1024]{1,0:T(8,128)S(1)}, u32[]{:S(2)}, u32[]{:S(2)}) %collective-permute-start) | collective-permute-done | bytes 65568 | tf_op jit(solution)/shard_map/ppermute | solution.py:32
  121.1 7.9 %collective-permute-done.1 = f32[16,1024]{1,0:T(8,128)S(1)} collective-permute-done((f32[16,1024]{1,0:T(8,128)S(1)}, f32[16,1024]{1,0:T(8,128)S(1)}, u32[]{:S(2)}, u32[]{:S(2)}) %collective-permute-start.1) | collective-permute-done | bytes 65568 | tf_op jit(solution)/shard_map/ppermute | solution.py:32
  129.0 7.9 %collective-permute-done.2 = f32[16,1024]{1,0:T(8,128)S(1)} collective-permute-done((f32[16,1024]{1,0:T(8,128)S(1)}, f32[16,1024]{1,0:T(8,128)S(1)}, u32[]{:S(2)}, u32[]{:S(2)}) %collective-permute-start.2) | collective-permute-done | bytes 65568 | tf_op jit(solution)/shard_map/ppermute | solution.py:32
  136.8 7.9 %collective-permute-done.3 = f32[16,1024]{1,0:T(8,128)S(1)} collective-permute-done((f32[16,1024]{1,0:T(8,128)S(1)}, f32[16,1024]{1,0:T(8,128)S(1)}, u32[]{:S(2)}, u32[]{:S(2)}) %collective-permute-start.3) | collective-permute-done | bytes 65568 | tf_op jit(solution)/shard_map/ppermute | solution.py:32
  144.7 7.9 %collective-permute-done.4 = f32[16,1024]{1,0:T(8,128)S(1)} collective-permute-done((f32[16,1024]{1,0:T(8,128)S(1)}, f32[16,1024]{1,0:T(8,128)S(1)}, u32[]{:S(2)}, u32[]{:S(2)}) %collective-permute-start.4) | collective-permute-done | bytes 65568 | tf_op jit(solution)/shard_map/ppermute | solution.py:32
  152.6 8.4 %collective-permute-done.5 = f32[16,1024]{1,0:T(8,128)S(1)} collective-permute-done((f32[16,1024]{1,0:T(8,128)S(1)}, f32[16,1024]{1,0:T(8,128)S(1)}, u32[]{:S(2)}, u32[]{:S(2)}) %collective-permute-start.5) | collective-permute-done | bytes 65568 | tf_op jit(solution)/shard_map/ppermute | solution.py:32
  161.0 8.3 %collective-permute-done.6 = f32[16,1024]{1,0:T(8,128)S(1)} collective-permute-done((f32[16,1024]{1,0:T(8,128)S(1)}, f32[16,1024]{1,0:T(8,128)S(1)}, u32[]{:S(2)}, u32[]{:S(2)}) %collective-permute-start.6) | collective-permute-done | bytes 65568 | tf_op jit(solution)/shard_map/ppermute | solution.py:32
  169.9 7.9 %collective-permute-done.7 = f32[16,1024]{1,0:T(8,128)S(1)} collective-permute-done((f32[16,1024]{1,0:T(8,128)S(1)}, f32[16,1024]{1,0:T(8,128)S(1)}, u32[]{:S(2)}, u32[]{:S(2)}) %collective-permute-start.7) | collective-permute-done | bytes 65568 | tf_op jit(solution)/shard_map/ppermute | solution.py:32
  178.4 7.9 %collective-permute-done.8 = f32[16,1024]{1,0:T(8,128)S(1)} collective-permute-done((f32[16,1024]{1,0:T(8,128)S(1)}, f32[16,1024]{1,0:T(8,128)S(1)}, u32[]{:S(2)}, u32[]{:S(2)}) %collective-permute-start.8) | collective-permute-done | bytes 65568 | tf_op jit(solution)/shard_map/ppermute | solution.py:32
  186.9 7.9 %collective-permute-done.9 = f32[16,1024]{1,0:T(8,128)S(1)} collective-permute-done((f32[16,1024]{1,0:T(8,128)S(1)}, f32[16,1024]{1,0:T(8,128)S(1)}, u32[]{:S(2)}, u32[]{:S(2)}) %collective-permute-start.9) | collective-permute-done | bytes 65568 | tf_op jit(solution)/shard_map/ppermute | solution.py:32
  195.4 7.9 %collective-permute-done.10 = f32[16,1024]{1,0:T(8,128)S(1)} collective-permute-done((f32[16,1024]{1,0:T(8,128)S(1)}, f32[16,1024]{1,0:T(8,128)S(1)}, u32[]{:S(2)}, u32[]{:S(2)}) %collective-permute-start.10) | collective-permute-done | bytes 65568 | tf_op jit(solution)/shard_map/ppermute | solution.py:32
  203.8 7.9 %collective-permute-done.11 = f32[16,1024]{1,0:T(8,128)S(1)} collective-permute-done((f32[16,1024]{1,0:T(8,128)S(1)}, f32[16,1024]{1,0:T(8,128)S(1)}, u32[]{:S(2)}, u32[]{:S(2)}) %collective-permute-start.11) | collective-permute-done | bytes 65568 | tf_op jit(solution)/shard_map/ppermute | solution.py:32
  212.3 8.4 %collective-permute-done.12 = f32[16,1024]{1,0:T(8,128)S(1)} collective-permute-done((f32[16,1024]{1,0:T(8,128)S(1)}, f32[16,1024]{1,0:T(8,128)S(1)}, u32[]{:S(2)}, u32[]{:S(2)}) %collective-permute-start.12) | collective-permute-done | bytes 65568 | tf_op jit(solution)/shard_map/ppermute | solution.py:32
  221.3 8.0 %collective-permute-done.13 = f32[16,1024]{1,0:T(8,128)} collective-permute-done((f32[16,1024]{1,0:T(8,128)S(1)}, f32[16,1024]{1,0:T(8,128)}, u32[]{:S(2)}, u32[]{:S(2)}) %collective-permute-start.13) | collective-permute-done | bytes 65568 | tf_op jit(solution)/shard_map/ppermute | solution.py:32
  229.4 8.1 %collective-permute-done.14 = f32[16,1024]{1,0:T(8,128)} collective-permute-done((f32[16,1024]{1,0:T(8,128)}, f32[16,1024]{1,0:T(8,128)}, u32[]{:S(2)}, u32[]{:S(2)}) %collective-permute-start.14) | collective-permute-done | bytes 65568 | tf_op jit(solution)/shard_map/ppermute | solution.py:32
  237.5 0.8 constant_dynamic-update-slice_fusion.31
  238.3 0.8 constant_dynamic-update-slice_fusion.30
  239.2 0.8 constant_dynamic-update-slice_fusion.29
  242.6 0.8 constant_dynamic-update-slice_fusion.25
  245.2 0.8 constant_dynamic-update-slice_fusion.15
  247.2 1.4 copy-done.1
  248.5 14.2 %fusion.1 = f32[256,2992]{0,1:T(8,128)} fusion(f32[1024,2992]{0,1:T(8,128)} %param.4, f32[512,1024]{1,0:T(8,128)S(1)} %constant_dynamic-update-slice_fusion, s32[]{:T(128)S(6)} %select_n.14), kind=kOutput, calls=%fused_computation.2 | convolution fusion | flops 9412018176 | bytes 16367620 | tf_op jit(solution)/shard_map/dot_general | solution.py:43
  262.7 14.0 %convolution_multiply_fusion = f32[1024,2992]{0,1:T(8,128)} fusion(f32[256,2992]{0,1:T(8,128)S(1)} %copy-done, f32[512,1024]{1,0:T(8,128)} %copy-done.1, s32[]{:T(128)S(6)} %select_n.14), kind=kOutput, calls=%fused_computation | convolution fusion | flops 9415081984 | bytes 16367620 | tf_op jit(solution)/shard_map/dot_general | solution.py:36
  276.7 2.7 broadcast_multiply_fusion
  (79 shorter events, 9.9 us)
Async XLA Ops:
  7.2 1.9 copy-start
  7.2 105.1 %copy-start.16 = (f32[16,1024]{1,0:T(8,128)S(1)}, f32[16,1024]{1,0:T(8,128)}, u32[]{:S(2)}) copy-start(f32[16,1024]{1,0:T(8,128)} %param.5) | copy-start | bytes 196612
  7.2 98.1 %reduce-scatter.3.cloned.1.call-start = ((), (), s32[]{:S(2)}) async-start(), calls=%async_computation.2 | async-start | bytes 1114112 | tf_op jit(solution)/shard_map/reduce_scatter | solution.py:21
  23.7 253.1 %reduce-scatter.5.cloned.1.call-start = ((), (), s32[]{:S(2)}) async-start(), calls=%async_computation.3 | async-start | bytes 4595712 | tf_op jit(solution)/shard_map/reduce_scatter | solution.py:46
  113.2 7.9 %collective-permute-start = (f32[16,1024]{1,0:T(8,128)S(1)}, f32[16,1024]{1,0:T(8,128)S(1)}, u32[]{:S(2)}, u32[]{:S(2)}) collective-permute-start(f32[16,1024]{1,0:T(8,128)S(1)} %subtract_multiply_fusion), channel_id=1, source_target_pairs={{0,2},{2,4},{4,6},{6,8},{8,10},{10,12},{12,14},{14,16},{16,18},{18... | collective-permute-start | bytes 196616 | tf_op jit(solution)/shard_map/ppermute | solution.py:32
  121.1 7.9 %collective-permute-start.1 = (f32[16,1024]{1,0:T(8,128)S(1)}, f32[16,1024]{1,0:T(8,128)S(1)}, u32[]{:S(2)}, u32[]{:S(2)}) collective-permute-start(f32[16,1024]{1,0:T(8,128)S(1)} %collective-permute-done), channel_id=1, source_target_pairs={{0,2},{2,4},{4,6},{6,8},{8,10},{10,12},{12,14},{14,16},{16,18},{18... | collective-permute-start | bytes 196616 | tf_op jit(solution)/shard_map/ppermute | solution.py:32
  129.0 7.9 %collective-permute-start.2 = (f32[16,1024]{1,0:T(8,128)S(1)}, f32[16,1024]{1,0:T(8,128)S(1)}, u32[]{:S(2)}, u32[]{:S(2)}) collective-permute-start(f32[16,1024]{1,0:T(8,128)S(1)} %collective-permute-done.1), channel_id=1, source_target_pairs={{0,2},{2,4},{4,6},{6,8},{8,10},{10,12},{12,14},{14,16},{16,18},{18... | collective-permute-start | bytes 196616 | tf_op jit(solution)/shard_map/ppermute | solution.py:32
  136.8 7.9 %collective-permute-start.3 = (f32[16,1024]{1,0:T(8,128)S(1)}, f32[16,1024]{1,0:T(8,128)S(1)}, u32[]{:S(2)}, u32[]{:S(2)}) collective-permute-start(f32[16,1024]{1,0:T(8,128)S(1)} %collective-permute-done.2), channel_id=1, source_target_pairs={{0,2},{2,4},{4,6},{6,8},{8,10},{10,12},{12,14},{14,16},{16,18},{18... | collective-permute-start | bytes 196616 | tf_op jit(solution)/shard_map/ppermute | solution.py:32
  144.7 7.9 %collective-permute-start.4 = (f32[16,1024]{1,0:T(8,128)S(1)}, f32[16,1024]{1,0:T(8,128)S(1)}, u32[]{:S(2)}, u32[]{:S(2)}) collective-permute-start(f32[16,1024]{1,0:T(8,128)S(1)} %collective-permute-done.3), channel_id=1, source_target_pairs={{0,2},{2,4},{4,6},{6,8},{8,10},{10,12},{12,14},{14,16},{16,18},{18... | collective-permute-start | bytes 196616 | tf_op jit(solution)/shard_map/ppermute | solution.py:32
  152.6 8.4 %collective-permute-start.5 = (f32[16,1024]{1,0:T(8,128)S(1)}, f32[16,1024]{1,0:T(8,128)S(1)}, u32[]{:S(2)}, u32[]{:S(2)}) collective-permute-start(f32[16,1024]{1,0:T(8,128)S(1)} %collective-permute-done.4), channel_id=1, source_target_pairs={{0,2},{2,4},{4,6},{6,8},{8,10},{10,12},{12,14},{14,16},{16,18},{18... | collective-permute-start | bytes 196616 | tf_op jit(solution)/shard_map/ppermute | solution.py:32
  160.9 8.3 %collective-permute-start.6 = (f32[16,1024]{1,0:T(8,128)S(1)}, f32[16,1024]{1,0:T(8,128)S(1)}, u32[]{:S(2)}, u32[]{:S(2)}) collective-permute-start(f32[16,1024]{1,0:T(8,128)S(1)} %collective-permute-done.5), channel_id=1, source_target_pairs={{0,2},{2,4},{4,6},{6,8},{8,10},{10,12},{12,14},{14,16},{16,18},{18... | collective-permute-start | bytes 196616 | tf_op jit(solution)/shard_map/ppermute | solution.py:32
  169.9 7.9 %collective-permute-start.7 = (f32[16,1024]{1,0:T(8,128)S(1)}, f32[16,1024]{1,0:T(8,128)S(1)}, u32[]{:S(2)}, u32[]{:S(2)}) collective-permute-start(f32[16,1024]{1,0:T(8,128)S(1)} %collective-permute-done.6), channel_id=1, source_target_pairs={{0,2},{2,4},{4,6},{6,8},{8,10},{10,12},{12,14},{14,16},{16,18},{18... | collective-permute-start | bytes 196616 | tf_op jit(solution)/shard_map/ppermute | solution.py:32
  178.4 7.9 %collective-permute-start.8 = (f32[16,1024]{1,0:T(8,128)S(1)}, f32[16,1024]{1,0:T(8,128)S(1)}, u32[]{:S(2)}, u32[]{:S(2)}) collective-permute-start(f32[16,1024]{1,0:T(8,128)S(1)} %collective-permute-done.7), channel_id=1, source_target_pairs={{0,2},{2,4},{4,6},{6,8},{8,10},{10,12},{12,14},{14,16},{16,18},{18... | collective-permute-start | bytes 196616 | tf_op jit(solution)/shard_map/ppermute | solution.py:32
  186.2 0.6 copy-start.6
  186.9 7.9 %collective-permute-start.9 = (f32[16,1024]{1,0:T(8,128)S(1)}, f32[16,1024]{1,0:T(8,128)S(1)}, u32[]{:S(2)}, u32[]{:S(2)}) collective-permute-start(f32[16,1024]{1,0:T(8,128)S(1)} %collective-permute-done.8), channel_id=1, source_target_pairs={{0,2},{2,4},{4,6},{6,8},{8,10},{10,12},{12,14},{14,16},{16,18},{18... | collective-permute-start | bytes 196616 | tf_op jit(solution)/shard_map/ppermute | solution.py:32
  194.7 0.6 copy-start.8
  195.4 7.9 %collective-permute-start.10 = (f32[16,1024]{1,0:T(8,128)S(1)}, f32[16,1024]{1,0:T(8,128)S(1)}, u32[]{:S(2)}, u32[]{:S(2)}) collective-permute-start(f32[16,1024]{1,0:T(8,128)S(1)} %collective-permute-done.9), channel_id=1, source_target_pairs={{0,2},{2,4},{4,6},{6,8},{8,10},{10,12},{12,14},{14,16},{16,18},{18... | collective-permute-start | bytes 196616 | tf_op jit(solution)/shard_map/ppermute | solution.py:32
  203.2 0.6 copy-start.10
  203.8 7.9 %collective-permute-start.11 = (f32[16,1024]{1,0:T(8,128)S(1)}, f32[16,1024]{1,0:T(8,128)S(1)}, u32[]{:S(2)}, u32[]{:S(2)}) collective-permute-start(f32[16,1024]{1,0:T(8,128)S(1)} %collective-permute-done.10), channel_id=1, source_target_pairs={{0,2},{2,4},{4,6},{6,8},{8,10},{10,12},{12,14},{14,16},{16,18},{18... | collective-permute-start | bytes 196616 | tf_op jit(solution)/shard_map/ppermute | solution.py:32
  211.7 0.6 copy-start.12
  212.3 8.4 %collective-permute-start.12 = (f32[16,1024]{1,0:T(8,128)S(1)}, f32[16,1024]{1,0:T(8,128)S(1)}, u32[]{:S(2)}, u32[]{:S(2)}) collective-permute-start(f32[16,1024]{1,0:T(8,128)S(1)} %collective-permute-done.11), channel_id=1, source_target_pairs={{0,2},{2,4},{4,6},{6,8},{8,10},{10,12},{12,14},{14,16},{16,18},{18... | collective-permute-start | bytes 196616 | tf_op jit(solution)/shard_map/ppermute | solution.py:32
  220.7 0.6 copy-start.14
  221.3 8.0 %collective-permute-start.13 = (f32[16,1024]{1,0:T(8,128)S(1)}, f32[16,1024]{1,0:T(8,128)}, u32[]{:S(2)}, u32[]{:S(2)}) collective-permute-start(f32[16,1024]{1,0:T(8,128)S(1)} %collective-permute-done.12), channel_id=1, source_target_pairs={{0,2},{2,4},{4,6},{6,8},{8,10},{10,12},{12,14},{14,16},{16,18},{18... | collective-permute-start | bytes 196616 | tf_op jit(solution)/shard_map/ppermute | solution.py:32
  229.3 8.2 %collective-permute-start.14 = (f32[16,1024]{1,0:T(8,128)}, f32[16,1024]{1,0:T(8,128)}, u32[]{:S(2)}, u32[]{:S(2)}) collective-permute-start(f32[16,1024]{1,0:T(8,128)} %collective-permute-done.13), channel_id=1, source_target_pairs={{0,2},{2,4},{4,6},{6,8},{8,10},{10,12},{12,14},{14,16},{16,18},{18... | collective-permute-start | bytes 196616 | tf_op jit(solution)/shard_map/ppermute | solution.py:32
  229.3 17.6 %copy-start.15 = (f32[16,1024]{1,0:T(8,128)S(1)}, f32[16,1024]{1,0:T(8,128)}, u32[]{:S(2)}) copy-start(f32[16,1024]{1,0:T(8,128)} %copy-done.14) | copy-start | bytes 196612
  229.3 17.6 %copy-start.13 = (f32[16,1024]{1,0:T(8,128)S(1)}, f32[16,1024]{1,0:T(8,128)}, u32[]{:S(2)}) copy-start(f32[16,1024]{1,0:T(8,128)} %copy-done.12) | copy-start | bytes 196612
  229.3 17.6 %copy-start.11 = (f32[16,1024]{1,0:T(8,128)S(1)}, f32[16,1024]{1,0:T(8,128)}, u32[]{:S(2)}) copy-start(f32[16,1024]{1,0:T(8,128)} %copy-done.10) | copy-start | bytes 196612
  229.3 17.6 %copy-start.9 = (f32[16,1024]{1,0:T(8,128)S(1)}, f32[16,1024]{1,0:T(8,128)}, u32[]{:S(2)}) copy-start(f32[16,1024]{1,0:T(8,128)} %copy-done.8) | copy-start | bytes 196612
  229.3 17.6 %copy-start.7 = (f32[16,1024]{1,0:T(8,128)S(1)}, f32[16,1024]{1,0:T(8,128)}, u32[]{:S(2)}) copy-start(f32[16,1024]{1,0:T(8,128)} %copy-done.6) | copy-start | bytes 196612
  229.3 17.6 %copy-start.5 = (f32[16,1024]{1,0:T(8,128)S(1)}, f32[16,1024]{1,0:T(8,128)}, u32[]{:S(2)}) copy-start(f32[16,1024]{1,0:T(8,128)} %copy-done.4) | copy-start | bytes 196612
  229.4 17.7 %copy-start.3 = (f32[16,1024]{1,0:T(8,128)S(1)}, f32[16,1024]{1,0:T(8,128)}, u32[]{:S(2)}) copy-start(f32[16,1024]{1,0:T(8,128)} %copy-done.2) | copy-start | bytes 196612
  247.1 1.4 copy-start.1
  (2 other events, 1.2 us)
Sparse Core Ops, SparseCore 0:
  23.8 81.4 reduce-scatter.2
  262.8 6.7 reduce-scatter.4
